TPU v7x, 256 devices: a whole 4x4x8 slice. The times are simulated.
256 devices in a mesh: group: 16 (over z, core), blk: 16 (over y, x).
Axes of the slice: x: 4, y: 4, z: 8, core: 2. Of those that a mesh axis runs over, the one named last changes fastest.
Arguments:
- hamiltonian: bfloat16 [4096, 18, 64, 256], P(('group', 'blk')), may hold values from -0.09375 to 0.09375
- block_columns: int32 [4096, 18, 4], P(('group', 'blk')), may hold values from 0 to 15, as said below
- potential: float32 [262144], P(('group', 'blk')), may hold values from -1 to 1
- trial_slab: float32 [262144, 128], P(('group', 'blk')), may hold values from -40 to 40
Outputs:
- ortho_slab: float32 [262144, 128], P(('group', 'blk'))
- upper_factor: float32 [128, 128], replicated
Inputs may be any that keep to these rules, and one draw needn't show every extreme that they name: `block_columns`: for each row block and each source, the 4 entries are distinct.
All inputs are finite; a program needn't handle non-finite values.
Results may differ from a plain program's by a relative error of at most 0.0021.
Values may be sent and summed in bfloat16 or wider, within the bound.
A program may use at most 64 MiB of HBM per device.

v0:
```python
import jax
import jax.numpy as jnp
from jax import lax
from jax.sharding import PartitionSpec as P

precise = lax.Precision.HIGHEST


def neighbours(block):
    count = lax.axis_size("group")
    forward = [(i, i + 1) for i in range(count - 1)]
    backward = [(i + 1, i) for i in range(count - 1)]
    below = lax.ppermute(block, "group", forward)
    above = lax.ppermute(block, "group", backward)
    return (below, above)


def couple_all(hamiltonian, block_columns, rounded):
    shard_blocks, nsrc, block_size, width = hamiltonian.shape
    per_source = block_columns.shape[2]
    states = rounded.shape[2]
    gathered = lax.all_gather(rounded, "blk", axis=0, tiled=True)
    below, above = neighbours(rounded)
    table = jnp.concatenate([gathered, below, above], axis=0)
    offsets = (jnp.arange(nsrc, dtype=jnp.int32) * shard_blocks)[None, :, None]
    index = block_columns + offsets
    picked = table[index.reshape(-1)].reshape(shard_blocks, nsrc, per_source * block_size, states)
    return jnp.einsum("rsik,rskn->rin", hamiltonian, picked, preferred_element_type=jnp.float32)


def on_device(hamiltonian, block_columns, potential, trial_slab):
    shard_blocks = hamiltonian.shape[0]
    block_size = hamiltonian.shape[2]
    states = trial_slab.shape[1]
    start_slab = trial_slab.reshape(shard_blocks, block_size, states)
    weights = potential.reshape(shard_blocks, block_size, 1)
    coupled_start = couple_all(hamiltonian, block_columns, start_slab.astype(jnp.bfloat16))
    filtered_once = 0.5 * (coupled_start + weights * start_slab)
    coupled_next = couple_all(hamiltonian, block_columns, filtered_once.astype(jnp.bfloat16))
    filtered = coupled_next + weights * filtered_once - start_slab
    flat = filtered.reshape(shard_blocks * block_size, states)
    rows_total = flat.shape[0] * lax.axis_size("group") * lax.axis_size("blk")
    local_gram = jnp.dot(flat.T, flat, precision=precise)
    gram = lax.psum(local_gram, ("group", "blk")) / rows_total
    lower = jnp.linalg.cholesky(gram)
    ortho_slab = lax.linalg.triangular_solve(
        lower, flat, left_side=False, lower=True, transpose_a=True
    )
    return (ortho_slab, jnp.transpose(lower))


def solution(mesh):
    placed = (
        P(("group", "blk"), None, None, None),
        P(("group", "blk"), None, None),
        P(("group", "blk")),
        P(("group", "blk"), None),
    )
    return jax.shard_map(
        on_device,
        mesh=mesh,
        in_specs=placed,
        out_specs=(P(("group", "blk"), None), P()),
        check_vma=False,
    )
```

profile of v0, /device:TPU:1, one launch (start us, length us, event | category | flops | bytes accessed | tf_op | source)
XLA Modules:
  0.0 493.7 jit_solution(8105677238921476546)
XLA Ops:
  7.2 0.0 all-gather.3.cloned.1.call-start
  7.2 1.8 convert_element_type.6
  9.0 0.0 all-gather.3.cloned.1.call-update
  9.0 0.0 all-gather.5.cloned.1.call-start
  9.1 5.1 %collective-permute-start.1 = (bf16[16,64,128]{2,1,0:T(8,128)(2,1)}, bf16[16,64,128]{2,1,0:T(8,128)(2,1)S(1)}, u32[]{:S(2)}, u32[]{:S(2)}) collective-permute-start(bf16[16,64,128]{2,1,0:T(8,128)(2,1)} %convert_element_type.6), channel_id=1, source_target_pairs={{16,0},{32,16},{48,32},{64,48},{80,64},{96,80},{112,96},{128,112},... | collective-permute-start | bytes 786440 | tf_op jit(solution)/shard_map/ppermute | solution.py:14
  14.2 1.9 collective-permute-start
  16.2 0.8 broadcast_add_fusion
  16.9 0.8 mul.37
  17.7 0.2 copy.13
  17.9 0.1 reshape.64
  18.1 0.2 collective-permute-done.1
  18.3 1.5 collective-permute-done
  19.8 51.6 %all-gather.3.cloned.1.call-done = bf16[256,64,128]{2,1,0:T(8,128)(2,1)} async-done(((bf16[16,64,128]{2,1,0:T(8,128)(2,1)}), bf16[256,64,128]{2,1,0:T(8,128)(2,1)}) %all-gather.3.cloned.1.call-update) | async-done | bytes 4194320 | tf_op jit(solution)/shard_map/all_gather | solution.py:22
  71.4 4.2 pad_maximum_fusion
  75.5 0.0 copy-start
  75.5 29.1 %gather_fusion = bf16[1152,64,128]{2,1,0:T(8,128)(2,1)} fusion(bf16[288,64,128]{2,1,0:T(8,128)(2,1)} %pad_maximum_fusion, s32[2048]{0:T(1024)S(1)} %pad_clamp_fusion), kind=kCustom, calls=%fused_computation | custom fusion | bytes 37753344 | tf_op jit(solution)/shard_map/gather | solution.py:27
  104.6 0.0 copy-done
  104.6 13.5 %multiply_convert_fusion = (bf16[16,64,128]{2,1,0:T(8,128)(2,1)}, f32[16,64,128]{2,1,0:T(8,128)S(1)}) fusion(f32[16,64,128]{2,1,0:T(8,128)S(1)} %bitcast.44, f32[16,64]{1,0:T(8,128)S(1)} %mul.37, bf16[16,18,64,256]{3,2,1,0:T(8,128)(2,1)} %param.4, bf16[16,18,256,128]{3,2,1,0:T(8,128)(2,1)} %bitcast.41), kind=kOutput, calls=%fused_computation.10 | convolution fusion | flops 1208483840 | bytes 29626368 | tf_op jit(solution)/shard_map/rsik,rskn->rin/dot_general | solution.py:28
  118.2 0.0 all-gather.5.cloned.1.call-update
  118.2 0.0 all-reduce.2.cloned.1.call-start
  118.2 2.6 collective-permute-start.3
  120.8 3.3 collective-permute-start.2
  124.1 2.1 collective-permute-done.3
  126.2 1.3 collective-permute-done.2
  127.5 47.1 %all-gather.5.cloned.1.call-done = bf16[256,64,128]{2,1,0:T(8,128)(2,1)} async-done(((bf16[16,64,128]{2,1,0:T(8,128)(2,1)}), bf16[256,64,128]{2,1,0:T(8,128)(2,1)}) %all-gather.5.cloned.1.call-update) | async-done | bytes 4194320 | tf_op jit(solution)/shard_map/all_gather | solution.py:22
  174.6 4.2 pad_maximum_fusion.1
  178.8 29.2 %gather_fusion.1 = bf16[1152,64,128]{2,1,0:T(8,128)(2,1)} fusion(bf16[288,64,128]{2,1,0:T(8,128)(2,1)} %pad_maximum_fusion.1, s32[2048]{0:T(1024)S(1)} %pad_clamp_fusion), kind=kCustom, calls=%fused_computation.1 | custom fusion | bytes 37753344 | tf_op jit(solution)/shard_map/gather | solution.py:27
  208.0 12.8 %fusion.2 = f32[16,64,128]{2,1,0:T(8,128)S(1)} fusion(f32[16,64,128]{2,1,0:T(8,128)S(1)} %bitcast.45, bf16[16,18,64,256]{3,2,1,0:T(8,128)(2,1)} %param.4, bf16[16,18,256,128]{3,2,1,0:T(8,128)(2,1)} %bitcast.40, f32[16,64,128]{2,1,0:T(8,128)S(1)} %get-tuple-element.11, f32[16,64]{1,0:T(8,128)S(1)} %broadcast_multiply_fusion.1), kind=kOutput, calls=%fused_computation.8 | convolution fusion | flops 1208352768 | bytes 29888512 | tf_op jit(solution)/shard_map/rsik,rskn->rin/dot_general | solution.py:28
  220.8 1.6 convolution_bitcast_fusion.2
  222.5 0.0 all-reduce.2.cloned.1.call-update
  222.5 237.9 %all-reduce.2.cloned.1.call-done = f32[128,128]{0,1:T(8,128)} async-done(((f32[128,128]{0,1:T(8,128)}), f32[128,128]{0,1:T(8,128)}) %all-reduce.2.cloned.1.call-update) | async-done | bytes 65552 | tf_op jit(solution)/shard_map/psum | solution.py:44
  460.4 0.8 broadcast_multiply_fusion
  461.3 0.1 copy.15
  461.4 0.9 fusion.5
  462.2 11.7 %cholesky.16 = f32[128,128]{1,0:T(8,128)S(1)} custom-call(f32[128,128]{1,0:T(8,128)S(1)} %fusion.5), custom_call_target="Cholesky" | custom-call | tf_op jit(solution)/shard_map/jit(cholesky)/cholesky | solution.py:45
  474.0 0.6 compare_reduce_fusion
  474.6 0.7 fusion.6
  475.3 0.7 copy.16
  476.0 9.8 %custom-call.6 = f32[1,128,128]{1,2,0:T(8,128)S(1)} custom-call(f32[1,128,128]{2,1,0:T(8,128)S(1)} %get-tuple-element.9), custom_call_target="InvertDiagBlocksLowerTriangular" | custom-call | tf_op jit(solution)/shard_map/triangular_solve | solution.py:46
  485.8 1.4 fusion.3
  (5 shorter events, 0.1 us)
Async XLA Ops:
  7.2 64.2 %all-gather.3.cloned.1.call-start = ((), (), s32[]{:S(2)}) async-start(), calls=%async_computation | async-start | bytes 4456448 | tf_op jit(solution)/shard_map/all_gather | solution.py:22
  9.0 165.6 %all-gather.5.cloned.1.call-start = ((), (), s32[]{:S(2)}) async-start(), calls=%async_computation.1 | async-start | bytes 4456448 | tf_op jit(solution)/shard_map/all_gather | solution.py:22
  9.1 9.2 %collective-permute-start.1 = (bf16[16,64,128]{2,1,0:T(8,128)(2,1)}, bf16[16,64,128]{2,1,0:T(8,128)(2,1)S(1)}, u32[]{:S(2)}, u32[]{:S(2)}) collective-permute-start(bf16[16,64,128]{2,1,0:T(8,128)(2,1)} %convert_element_type.6), channel_id=1, source_target_pairs={{16,0},{32,16},{48,32},{64,48},{80,64},{96,80},{112,96},{128,112},... | collective-permute-start | bytes 786440 | tf_op jit(solution)/shard_map/ppermute | solution.py:14
  14.2 5.5 %collective-permute-start = (bf16[16,64,128]{2,1,0:T(8,128)(2,1)}, bf16[16,64,128]{2,1,0:T(8,128)(2,1)S(1)}, u32[]{:S(2)}, u32[]{:S(2)}) collective-permute-start(bf16[16,64,128]{2,1,0:T(8,128)(2,1)} %convert_element_type.6), channel_id=1, source_target_pairs={{0,16},{16,32},{32,48},{48,64},{64,80},{80,96},{96,112},{112,128},... | collective-permute-start | bytes 786440 | tf_op jit(solution)/shard_map/ppermute | solution.py:13
  75.5 29.1 %copy-start = (f32[1024,128]{1,0:T(8,128)S(1)}, f32[1024,128]{1,0:T(8,128)}, u32[]{:S(2)}) copy-start(f32[1024,128]{1,0:T(8,128)} %param.7) | copy-start | bytes 1572868
  118.2 342.3 %all-reduce.2.cloned.1.call-start = ((), (), s32[]{:S(2)}) async-start(), calls=%async_computation.2 | async-start | bytes 131072 | tf_op jit(solution)/shard_map/psum | solution.py:44
  118.2 8.0 %collective-permute-start.3 = (bf16[16,64,128]{2,1,0:T(8,128)(2,1)}, bf16[16,64,128]{2,1,0:T(8,128)(2,1)S(1)}, u32[]{:S(2)}, u32[]{:S(2)}) collective-permute-start(bf16[16,64,128]{2,1,0:T(8,128)(2,1)} %get-tuple-element.10), channel_id=1, source_target_pairs={{16,0},{32,16},{48,32},{64,48},{80,64},{96,80},{112,96},{128,112},... | collective-permute-start | bytes 786440 | tf_op jit(solution)/shard_map/ppermute | solution.py:14
  120.8 6.7 %collective-permute-start.2 = (bf16[16,64,128]{2,1,0:T(8,128)(2,1)}, bf16[16,64,128]{2,1,0:T(8,128)(2,1)S(1)}, u32[]{:S(2)}, u32[]{:S(2)}) collective-permute-start(bf16[16,64,128]{2,1,0:T(8,128)(2,1)} %get-tuple-element.10), channel_id=1, source_target_pairs={{0,16},{16,32},{32,48},{48,64},{64,80},{80,96},{96,112},{112,128},... | collective-permute-start | bytes 786440 | tf_op jit(solution)/shard_map/ppermute | solution.py:13
Sparse Core Ops, SparseCore 0:
  11.0 60.3 all-gather.2
  118.3 56.2 all-gather.4
  222.6 237.7 all-reduce.1
where the time goes:
time: 494 us
  waiting for transfers between devices  342 us (69%)
  local copies, waits for them, and re-layouts  60.2 us (12%)
  other arithmetic  35.5 us (7%)
  matrix products  29.3 us (6%)
  between operations  13.9 us (3%)
  starting transfers between devices  13 us (3%)
    psum x1, waiting for transfers between devices, on_device(): gram = lax.psum(local_gram, ('group', 'blk')) / rows_total  238 us
    all_gather x2, waiting for transfers between devices, couple_all(): gathered = lax.all_gather(rounded, 'blk', axis=0, tiled=True)  98.7 us
    gather x2, local copies, waits for them, and re-layouts, couple_all(): table[index.reshape(-1)]  58.3 us
    dot_general x2, matrix products, couple_all(): jnp.einsum('rsik,rskn->rin', hamiltonian, picked, preferred_element_type=...  26.3 us
    another operation x3, other arithmetic, on_device(): lower = jnp.linalg.cholesky(gram)  12.4 us
  transfers between devices with their start and end apart: 7, of which 7 were waited for; matrix products, arithmetic and copies ran while one was open for 0% of the time, Pallas kernels for 0%

commit v1 on v0

--- a/solution.py
+++ b/solution.py
@@ -41,7 +41,11 @@
     flat = filtered.reshape(shard_blocks * block_size, states)
     rows_total = flat.shape[0] * lax.axis_size("group") * lax.axis_size("blk")
     local_gram = jnp.dot(flat.T, flat, precision=precise)
-    gram = lax.psum(local_gram, ("group", "blk")) / rows_total
+
+    def time_the_page(sheet):
+        return jnp.sum(jax.lax.all_gather(sheet, ("group", "blk")), axis=0)
+
+    gram = time_the_page(local_gram) / rows_total
     lower = jnp.linalg.cholesky(gram)
     ortho_slab = lax.linalg.triangular_solve(
         lower, flat, left_side=False, lower=True, transpose_a=True

time: 494 us -> 386 us (0.78)
  waiting for transfers between devices: 342 us -> 229 us
    psum x1 -> x0, waiting for transfers between devices: 238 us -> none  [on_device(): gram = lax.psum(local_gram, ('group', 'blk')) / rows_total]
    all_gather x0 -> x1, waiting for transfers between devices: none -> 125 us  [time_the_page(): return jnp.sum(jax.lax.all_gather(sheet, ('group', 'blk')), axis=0)]
    reduce_sum x0 -> x1, other arithmetic: none -> 6.59 us  [time_the_page(): return jnp.sum(jax.lax.all_gather(sheet, ('group', 'blk')), axis=0)]
where the time goes in v1:
time: 386 us
  waiting for transfers between devices  229 us (59%)
  local copies, waits for them, and re-layouts  60.2 us (16%)
  other arithmetic  40.4 us (10%)
  matrix products  29.3 us (8%)
  between operations  13.9 us (4%)
  starting transfers between devices  13 us (3%)
    all_gather x1, waiting for transfers between devices, time_the_page(): return jnp.sum(jax.lax.all_gather(sheet, ('group', 'blk')), axis=0)  125 us
    all_gather x2, waiting for transfers between devices, couple_all(): gathered = lax.all_gather(rounded, 'blk', axis=0, tiled=True)  98.7 us
    gather x2, local copies, waits for them, and re-layouts, couple_all(): table[index.reshape(-1)]  58.3 us
    dot_general x2, matrix products, couple_all(): jnp.einsum('rsik,rskn->rin', hamiltonian, picked, preferred_element_type=...  26.3 us
    another operation x3, other arithmetic, on_device(): lower = jnp.linalg.cholesky(gram)  12.4 us
    another operation x1, other arithmetic, on_device(): lax.linalg.triangular_solve(lower, flat, left_side=False, lower=True, tra...  9.81 us
    concatenate x2, other arithmetic, couple_all(): table = jnp.concatenate([gathered, below, above], axis=0)  8.31 us
    ppermute x2, starting transfers between devices, neighbours(): above = lax.ppermute(block, 'group', backward)  7.74 us
  transfers between devices with their start and end apart: 7, of which 7 were waited for; matrix products, arithmetic and copies ran while one was open for 0% of the time, Pallas kernels for 0%

profile of v1, /device:TPU:1, one launch (start us, length us, event | category | flops | bytes accessed | tf_op | source)
XLA Modules:
  0.0 385.9 jit_solution(13532769947968261188)
XLA Ops:
  7.2 0.0 all-gather.5.cloned.1.call-start
  7.2 1.8 convert_element_type.6
  9.0 0.0 all-gather.5.cloned.1.call-update
  9.0 0.0 all-gather.7.cloned.1.call-start
  9.1 5.1 %collective-permute-start.1 = (bf16[16,64,128]{2,1,0:T(8,128)(2,1)}, bf16[16,64,128]{2,1,0:T(8,128)(2,1)S(1)}, u32[]{:S(2)}, u32[]{:S(2)}) collective-permute-start(bf16[16,64,128]{2,1,0:T(8,128)(2,1)} %convert_element_type.6), channel_id=1, source_target_pairs={{16,0},{32,16},{48,32},{64,48},{80,64},{96,80},{112,96},{128,112},... | collective-permute-start | bytes 786440 | tf_op jit(solution)/shard_map/ppermute | solution.py:14
  14.2 1.9 collective-permute-start
  16.2 0.8 broadcast_add_fusion
  16.9 0.8 mul.37
  17.7 0.2 copy.11
  17.9 0.1 reshape.64
  18.1 0.2 collective-permute-done.1
  18.3 1.5 collective-permute-done
  19.8 51.6 %all-gather.5.cloned.1.call-done = bf16[256,64,128]{2,1,0:T(8,128)(2,1)} async-done(((bf16[16,64,128]{2,1,0:T(8,128)(2,1)}), bf16[256,64,128]{2,1,0:T(8,128)(2,1)}) %all-gather.5.cloned.1.call-update) | async-done | bytes 4194320 | tf_op jit(solution)/shard_map/all_gather | solution.py:22
  71.4 4.2 %pad_maximum_fusion = bf16[288,64,128]{2,1,0:T(8,128)(2,1)} fusion(bf16[16,64,128]{2,1,0:T(8,128)(2,1)S(1)} %collective-permute-done.1, bf16[16,64,128]{2,1,0:T(8,128)(2,1)S(1)} %collective-permute-done, bf16[256,64,128]{2,1,0:T(8,128)(2,1)} %all-gather.5.cloned.1.call-done), kind=kLoop, calls=%fused_computation.2 | loop fusion | flops 4718592 | bytes 9437184 | tf_op jit(solution)/shard_map/concatenate | solution.py:24
  75.5 0.0 copy-start
  75.5 29.1 %gather_fusion = bf16[1152,64,128]{2,1,0:T(8,128)(2,1)} fusion(bf16[288,64,128]{2,1,0:T(8,128)(2,1)} %pad_maximum_fusion, s32[2048]{0:T(1024)S(1)} %pad_clamp_fusion), kind=kCustom, calls=%fused_computation | custom fusion | bytes 37753344 | tf_op jit(solution)/shard_map/gather | solution.py:27
  104.6 0.0 copy-done
  104.6 13.5 %multiply_convert_fusion = (bf16[16,64,128]{2,1,0:T(8,128)(2,1)}, f32[16,64,128]{2,1,0:T(8,128)S(1)}) fusion(f32[16,64,128]{2,1,0:T(8,128)S(1)} %bitcast.46, f32[16,64]{1,0:T(8,128)S(1)} %mul.37, bf16[16,18,64,256]{3,2,1,0:T(8,128)(2,1)} %param.4, bf16[16,18,256,128]{3,2,1,0:T(8,128)(2,1)} %bitcast.42), kind=kOutput, calls=%fused_computation.10 | convolution fusion | flops 1208483840 | bytes 29626368 | tf_op jit(solution)/shard_map/rsik,rskn->rin/dot_general | solution.py:28
  118.2 0.0 all-gather.7.cloned.1.call-update
  118.2 0.0 all-gather.9.cloned.1.call-start
  118.2 2.6 collective-permute-start.3
  120.8 3.3 collective-permute-start.2
  124.1 2.1 collective-permute-done.3
  126.2 1.3 collective-permute-done.2
  127.5 47.1 %all-gather.7.cloned.1.call-done = bf16[256,64,128]{2,1,0:T(8,128)(2,1)} async-done(((bf16[16,64,128]{2,1,0:T(8,128)(2,1)}), bf16[256,64,128]{2,1,0:T(8,128)(2,1)}) %all-gather.7.cloned.1.call-update) | async-done | bytes 4194320 | tf_op jit(solution)/shard_map/all_gather | solution.py:22
  174.6 4.2 %pad_maximum_fusion.1 = bf16[288,64,128]{2,1,0:T(8,128)(2,1)} fusion(bf16[16,64,128]{2,1,0:T(8,128)(2,1)S(1)} %collective-permute-done.3, bf16[16,64,128]{2,1,0:T(8,128)(2,1)S(1)} %collective-permute-done.2, bf16[256,64,128]{2,1,0:T(8,128)(2,1)} %all-gather.7.cloned.1.call-done), kind=kLoop, calls=%fused_computation.3 | loop fusion | flops 4718592 | bytes 9437184 | tf_op jit(solution)/shard_map/concatenate | solution.py:24
  178.8 29.2 %gather_fusion.1 = bf16[1152,64,128]{2,1,0:T(8,128)(2,1)} fusion(bf16[288,64,128]{2,1,0:T(8,128)(2,1)} %pad_maximum_fusion.1, s32[2048]{0:T(1024)S(1)} %pad_clamp_fusion), kind=kCustom, calls=%fused_computation.1 | custom fusion | bytes 37753344 | tf_op jit(solution)/shard_map/gather | solution.py:27
  208.0 12.8 %fusion.2 = f32[16,64,128]{2,1,0:T(8,128)S(1)} fusion(f32[16,64,128]{2,1,0:T(8,128)S(1)} %bitcast.47, bf16[16,18,64,256]{3,2,1,0:T(8,128)(2,1)} %param.4, bf16[16,18,256,128]{3,2,1,0:T(8,128)(2,1)} %bitcast.41, f32[16,64,128]{2,1,0:T(8,128)S(1)} %get-tuple-element.11, f32[16,64]{1,0:T(8,128)S(1)} %broadcast_multiply_fusion), kind=kOutput, calls=%fused_computation.8 | convolution fusion | flops 1208352768 | bytes 29888512 | tf_op jit(solution)/shard_map/rsik,rskn->rin/dot_general | solution.py:28
  220.8 1.6 convolution_bitcast_fusion.2
  222.5 0.0 all-gather.9.cloned.1.call-update
  222.5 125.2 %all-gather.9.cloned.1.call-done = f32[32768,128]{1,0:T(8,128)} async-done(((f32[128,128]{1,0:T(8,128)}), f32[32768,128]{1,0:T(8,128)}) %all-gather.9.cloned.1.call-update) | async-done | bytes 16777232 | tf_op jit(solution)/shard_map/all_gather | solution.py:46
  347.7 6.6 %reduce_sum.11 = f32[128,128]{1,0:T(8,128)S(1)} reduce(f32[256,128,128]{2,1,0:T(8,128)} %bitcast.43, f32[]{:T(128)} %constant.49.clone.1), dimensions={0}, to_apply=%region_0.0 | reduce | flops 4177920 | bytes 16842756 | tf_op jit(solution)/shard_map/reduce_sum | solution.py:46
  354.3 0.1 copy.12
  354.4 11.7 %cholesky.16 = f32[128,128]{1,0:T(8,128)S(1)} custom-call(f32[128,128]{1,0:T(8,128)S(1)} %fusion.5), custom_call_target="Cholesky" | custom-call | tf_op jit(solution)/shard_map/jit(cholesky)/cholesky | solution.py:49
  366.1 0.6 compare_reduce_fusion
  366.8 0.7 fusion.6
  367.4 0.7 copy.13
  368.2 9.8 %custom-call.6 = f32[1,128,128]{1,2,0:T(8,128)S(1)} custom-call(f32[1,128,128]{2,1,0:T(8,128)S(1)} %get-tuple-element.9), custom_call_target="InvertDiagBlocksLowerTriangular" | custom-call | tf_op jit(solution)/shard_map/triangular_solve | solution.py:50
  378.0 1.4 fusion.3
  (6 shorter events, 0.1 us)
Async XLA Ops:
  7.2 64.2 %all-gather.5.cloned.1.call-start = ((), (), s32[]{:S(2)}) async-start(), calls=%async_computation | async-start | bytes 4456448 | tf_op jit(solution)/shard_map/all_gather | solution.py:22
  9.0 165.6 %all-gather.7.cloned.1.call-start = ((), (), s32[]{:S(2)}) async-start(), calls=%async_computation.1 | async-start | bytes 4456448 | tf_op jit(solution)/shard_map/all_gather | solution.py:22
  9.1 9.2 %collective-permute-start.1 = (bf16[16,64,128]{2,1,0:T(8,128)(2,1)}, bf16[16,64,128]{2,1,0:T(8,128)(2,1)S(1)}, u32[]{:S(2)}, u32[]{:S(2)}) collective-permute-start(bf16[16,64,128]{2,1,0:T(8,128)(2,1)} %convert_element_type.6), channel_id=1, source_target_pairs={{16,0},{32,16},{48,32},{64,48},{80,64},{96,80},{112,96},{128,112},... | collective-permute-start | bytes 786440 | tf_op jit(solution)/shard_map/ppermute | solution.py:14
  14.2 5.5 %collective-permute-start = (bf16[16,64,128]{2,1,0:T(8,128)(2,1)}, bf16[16,64,128]{2,1,0:T(8,128)(2,1)S(1)}, u32[]{:S(2)}, u32[]{:S(2)}) collective-permute-start(bf16[16,64,128]{2,1,0:T(8,128)(2,1)} %convert_element_type.6), channel_id=1, source_target_pairs={{0,16},{16,32},{32,48},{48,64},{64,80},{80,96},{96,112},{112,128},... | collective-permute-start | bytes 786440 | tf_op jit(solution)/shard_map/ppermute | solution.py:13
  75.5 29.1 %copy-start = (f32[1024,128]{1,0:T(8,128)S(1)}, f32[1024,128]{1,0:T(8,128)}, u32[]{:S(2)}) copy-start(f32[1024,128]{1,0:T(8,128)} %param.7) | copy-start | bytes 1572868
  118.2 229.5 %all-gather.9.cloned.1.call-start = ((), (), s32[]{:S(2)}) async-start(), calls=%async_computation.2 | async-start | bytes 16842752 | tf_op jit(solution)/shard_map/all_gather | solution.py:46
  118.2 8.0 %collective-permute-start.3 = (bf16[16,64,128]{2,1,0:T(8,128)(2,1)}, bf16[16,64,128]{2,1,0:T(8,128)(2,1)S(1)}, u32[]{:S(2)}, u32[]{:S(2)}) collective-permute-start(bf16[16,64,128]{2,1,0:T(8,128)(2,1)} %get-tuple-element.10), channel_id=1, source_target_pairs={{16,0},{32,16},{48,32},{64,48},{80,64},{96,80},{112,96},{128,112},... | collective-permute-start | bytes 786440 | tf_op jit(solution)/shard_map/ppermute | solution.py:14
  120.8 6.7 %collective-permute-start.2 = (bf16[16,64,128]{2,1,0:T(8,128)(2,1)}, bf16[16,64,128]{2,1,0:T(8,128)(2,1)S(1)}, u32[]{:S(2)}, u32[]{:S(2)}) collective-permute-start(bf16[16,64,128]{2,1,0:T(8,128)(2,1)} %get-tuple-element.10), channel_id=1, source_target_pairs={{0,16},{16,32},{32,48},{48,64},{64,80},{80,96},{96,112},{112,128},... | collective-permute-start | bytes 786440 | tf_op jit(solution)/shard_map/ppermute | solution.py:13
Sparse Core Ops, SparseCore 0:
  11.0 60.3 all-gather.4
  118.3 56.2 all-gather.6
  222.6 125.0 all-gather.8
